TPU v7x, 32 devices: a whole 2x2x4 slice. The times are simulated.
32 devices in a mesh: seq: 4 (over y, x), span: 4 (over z), kvg: 2 (over core).
Axes of the slice: x: 2, y: 2, z: 4, core: 2. Of those that a mesh axis runs over, the one named last changes fastest.
Arguments:
- query_rows: bfloat16 [8704, 1792], P(('seq', 'span'), 'kvg'), parts along dimension 0, may hold values from -256 to 256
- key_rows: bfloat16 [8704, 256], P(('seq', 'span'), 'kvg'), parts along dimension 0, may hold values from -6 to 6
- value_rows: bfloat16 [8704, 256], P(('seq', 'span'), 'kvg'), parts along dimension 0, may hold values from -6 to 6
- out_grad: bfloat16 [8704, 1792], P(('seq', 'span'), 'kvg'), parts along dimension 0, may hold values from -6 to 6
- ratios: int32 [16], P('seq'), parts along dimension 0, may hold values from 16 to 64, as said below
Outputs:
- attended: bfloat16 [8704, 1792], P(('seq', 'span'), 'kvg'), parts along dimension 0
- query_grad: bfloat16 [8704, 1792], P(('seq', 'span'), 'kvg'), parts along dimension 0
- key_grad: bfloat16 [8704, 256], P(('seq', 'span'), 'kvg'), parts along dimension 0
- value_grad: bfloat16 [8704, 256], P(('seq', 'span'), 'kvg'), parts along dimension 0
There are 4 independent parts, one for each index of `seq`. A program takes and returns all parts, laid end to end along the dimension named above; each array names one. Nothing has to cross between parts.
Inputs may be any that keep to these rules, and one draw needn't show every extreme that they name: `ratios`: every ratio is 16, 32 or 64, and some span of every sequence has 16.
All inputs are finite; a program needn't handle non-finite values.
Results may differ from a plain program's by a relative error of at most 0.0096.
Values may be sent and summed in bfloat16 or wider, within the bound.
A program may use at most 64 MiB of HBM per device.

v0:
```python
import jax
import jax.numpy as jnp
from jax import lax
from jax.sharding import PartitionSpec as P

SPAN = 512
HD = 128
QPG = 7
BMAX = 32
SEG = 544


floor_score = -1e30


def product(pattern, first_arg, second_arg):
    return jnp.einsum(pattern, first_arg, second_arg, preferred_element_type=jnp.float32)


def build_masks(ratios, first_span, local_spans):
    counts = SPAN // ratios
    slot_ids = jnp.arange(BMAX, dtype=jnp.int32)
    live_slots = (slot_ids[None, :] < counts[:, None]).reshape(-1)
    span_ids = first_span + jnp.arange(local_spans, dtype=jnp.int32)
    owner_span = jnp.arange(live_slots.shape[0], dtype=jnp.int32) // BMAX
    beacon_mask = (owner_span[None, :] < span_ids[:, None]) & live_slots[None, :]
    local_ratio = lax.dynamic_slice_in_dim(ratios, first_span, local_spans)
    local_count = SPAN // local_ratio
    positions = jnp.arange(SEG, dtype=jnp.int32)
    is_beacon = positions >= SPAN
    slot_of = positions - SPAN
    key_order = jnp.where(
        is_beacon[None, :], (slot_of[None, :] + 1) * local_ratio[:, None] - 1, positions[None, :]
    )
    live_row = jnp.logical_not(is_beacon[None, :]) | (slot_of[None, :] < local_count[:, None])
    raw_key = jnp.logical_not(is_beacon)[None, None, :] & (
        key_order[:, None, :] <= key_order[:, :, None]
    )
    beacon_key = (
        is_beacon[None, :, None]
        & is_beacon[None, None, :]
        & live_row[:, None, :]
        & (positions[None, None, :] <= positions[None, :, None])
    )
    return (beacon_mask, raw_key | beacon_key, live_row.astype(jnp.float32))


def attend_head(
    query_head,
    grad_head,
    beacon_keys,
    beacon_values,
    own_keys,
    own_values,
    beacon_mask,
    own_mask,
    live_rows,
):
    score_scale = HD ** (-0.5)
    beacon_scores = jnp.where(
        beacon_mask[:, None, :],
        product("csd,bd->csb", query_head, beacon_keys) * score_scale,
        floor_score,
    )
    own_scores = jnp.where(
        own_mask, product("csd,ctd->cst", query_head, own_keys) * score_scale, floor_score
    )
    row_top = jnp.maximum(jnp.max(beacon_scores, -1), jnp.max(own_scores, -1))
    row_total = jnp.sum(jnp.exp(beacon_scores - row_top[..., None]), -1) + jnp.sum(
        jnp.exp(own_scores - row_top[..., None]), -1
    )
    row_lse = row_top + jnp.log(row_total)
    beacon_probs = jnp.exp(beacon_scores - row_lse[..., None])
    own_probs = jnp.exp(own_scores - row_lse[..., None])
    beacon_weights = beacon_probs.astype(jnp.bfloat16)
    own_weights = own_probs.astype(jnp.bfloat16)
    mixed_rows = product("csb,bd->csd", beacon_weights, beacon_values) + product(
        "cst,ctd->csd", own_weights, own_values
    )
    attended = (mixed_rows * live_rows[..., None]).astype(jnp.bfloat16)
    grad_rows = grad_head * live_rows.astype(jnp.bfloat16)[..., None]
    row_delta = jnp.sum(grad_rows.astype(jnp.float32) * attended.astype(jnp.float32), -1)
    beacon_sgrad = (
        beacon_probs * (product("csd,bd->csb", grad_rows, beacon_values) - row_delta[..., None])
    ).astype(jnp.bfloat16)
    own_sgrad = (
        own_probs * (product("csd,ctd->cst", grad_rows, own_values) - row_delta[..., None])
    ).astype(jnp.bfloat16)
    query_grad = (
        score_scale
        * (
            product("csb,bd->csd", beacon_sgrad, beacon_keys)
            + product("cst,ctd->csd", own_sgrad, own_keys)
        )
    ).astype(jnp.bfloat16)
    beacon_kgrad = score_scale * product("csb,csd->bd", beacon_sgrad, query_head)
    beacon_vgrad = product("csb,csd->bd", beacon_weights, grad_rows)
    own_kgrad = score_scale * product("cst,csd->ctd", own_sgrad, query_head)
    own_vgrad = product("cst,csd->ctd", own_weights, grad_rows)
    return (attended, query_grad, beacon_kgrad, beacon_vgrad, own_kgrad, own_vgrad)


def local(query_rows, key_rows, value_rows, out_grad, ratios):
    span_index = lax.axis_index("span")
    local_spans = query_rows.shape[0] // SEG
    groups = key_rows.shape[1] // HD
    beacon_count = ratios.shape[0] * BMAX
    first_span = span_index * local_spans
    beacon_mask, own_mask, live_rows = build_masks(ratios, first_span, local_spans)
    query_blocks = query_rows.reshape(local_spans, SEG, groups, QPG, HD)
    grad_blocks = out_grad.reshape(local_spans, SEG, groups, QPG, HD)
    key_blocks = key_rows.reshape(local_spans, SEG, groups, HD)
    value_blocks = value_rows.reshape(local_spans, SEG, groups, HD)
    own_pair = jnp.concatenate(
        [
            key_blocks[:, SPAN:].reshape(local_spans * BMAX, groups * HD),
            value_blocks[:, SPAN:].reshape(local_spans * BMAX, groups * HD),
        ],
        1,
    )
    beacon_pairs = lax.all_gather(own_pair, "span", axis=0, tiled=True)
    attended_parts, query_parts, term_keys, term_values, own_key_parts, own_value_parts = (
        [],
        [],
        [],
        [],
        [],
        [],
    )
    own_keys = key_blocks[:, :, 0]
    own_values = value_blocks[:, :, 0]
    beacon_keys = beacon_pairs[:, 0:HD]
    beacon_values = beacon_pairs[:, groups * HD : (groups + 1) * HD]
    beacon_ksum = jnp.zeros((beacon_count, HD), jnp.float32)
    beacon_vsum = jnp.zeros((beacon_count, HD), jnp.float32)
    own_ksum = jnp.zeros((local_spans, SEG, HD), jnp.float32)
    own_vsum = jnp.zeros((local_spans, SEG, HD), jnp.float32)
    head_outputs = []
    head_grads = []
    for head_index in range(QPG):
        result = attend_head(
            query_blocks[:, :, 0, head_index],
            grad_blocks[:, :, 0, head_index],
            beacon_keys,
            beacon_values,
            own_keys,
            own_values,
            beacon_mask,
            own_mask,
            live_rows,
        )
        head_outputs.append(result[0])
        head_grads.append(result[1])
        beacon_ksum = beacon_ksum + result[2]
        beacon_vsum = beacon_vsum + result[3]
        own_ksum = own_ksum + result[4]
        own_vsum = own_vsum + result[5]
    attended_parts.append(jnp.stack(head_outputs, 2))
    query_parts.append(jnp.stack(head_grads, 2))
    term_keys.append(beacon_ksum)
    term_values.append(beacon_vsum)
    own_key_parts.append(own_ksum)
    own_value_parts.append(own_vsum)
    grad_term = jnp.concatenate(term_keys + term_values, 1)
    own_sums = lax.psum_scatter(grad_term, "span", scatter_dimension=0, tiled=True)
    own_sums = own_sums.reshape(local_spans, BMAX, 2 * groups, HD)
    own_key = jnp.stack(own_key_parts, 2)
    own_value = jnp.stack(own_value_parts, 2)
    key_total = jnp.concatenate([own_key[:, :SPAN], own_key[:, SPAN:] + own_sums[:, :, :groups]], 1)
    value_total = jnp.concatenate(
        [own_value[:, :SPAN], own_value[:, SPAN:] + own_sums[:, :, groups:]], 1
    )
    attended = jnp.stack(attended_parts, 2).reshape(local_spans * SEG, groups * QPG * HD)
    query_grad = jnp.stack(query_parts, 2).reshape(local_spans * SEG, groups * QPG * HD)
    key_grad = key_total.astype(jnp.bfloat16).reshape(local_spans * SEG, groups * HD)
    value_grad = value_total.astype(jnp.bfloat16).reshape(local_spans * SEG, groups * HD)
    return (attended, query_grad, key_grad, value_grad)


def solution(mesh):
    placed = (
        P(("seq", "span"), "kvg"),
        P(("seq", "span"), "kvg"),
        P(("seq", "span"), "kvg"),
        P(("seq", "span"), "kvg"),
        P("seq"),
    )
    return jax.shard_map(
        local,
        mesh=mesh,
        in_specs=placed,
        out_specs=(
            P(("seq", "span"), "kvg"),
            P(("seq", "span"), "kvg"),
            P(("seq", "span"), "kvg"),
            P(("seq", "span"), "kvg"),
        ),
        check_vma=False,
    )
```

profile of v0, /device:TPU:0, one launch (start us, length us, event | category | flops | bytes accessed | tf_op | source)
XLA Modules:
  0.0 112.2 jit_solution(4719098975755676397)
XLA Ops:
  7.2 1.2 %dynamic_slice.3 = s32[1]{0:T(128)} dynamic-slice(s32[4]{0:T(128)} %param.9, s32[]{:T(128)S(6)} %select_n.105), dynamic_slice_sizes={1} | dynamic-slice | bytes 12 | tf_op jit(solution)/shard_map/dynamic_slice | solution.py:27
  10.4 0.8 and_select_fusion
  11.3 0.7 iota_select_fusion
  11.9 2.2 %reshape.1308 = bf16[1,544,1,7,128]{4,3,1,2,0:T(8,128)(2,1)S(1)} reshape(bf16[544,896]{1,0:T(8,128)(2,1)} %param.5) | data formatting | bytes 1949696 | tf_op jit(solution)/shard_map/reshape | solution.py:110
  14.2 2.4 %fusion.265 = (bf16[1,544,1,1,128]{4,3,1,2,0:T(2,128)(2,1)S(1)}, bf16[1,544,1,1,128]{4,3,1,2,0:T(2,128)(2,1)S(1)}, bf16[1,544,1,1,128]{4,3,1,2,0:T(2,128)(2,1)},...) fusion(bf16[1,544,1,7,128]{4,3,1,2,0:T(8,128)(2,1)S(1)} %reshap, ...), kind=kLoop, calls=%fused_computation.404 | loop fusion | bytes 1949696 | tf_op jit(solution)/shard_map/slice | solution.py:142
  16.6 15.1 %all_gather.3 = bf16[128,256]{1,0:T(8,128)(2,1)S(1)} all-gather(bf16[32,256]{1,0:T(8,128)(2,1)S(1)} %pad_maximum_fusion.3), channel_id=1, replica_groups=mesh['seq'=4,'span'=4,'kvg'=2] {'span'}, dimensions={0}, use_global_device_ids=true | all-gather | bytes 81920 | tf_op jit(solution)/shard_map/all_gather | solution.py:121
  32.0 0.6 fusion.280
  32.6 1.4 %fusion.278 = (f32[544]{0:T(1024)S(1)}, f32[544,544]{0,1:T(8,128)S(1)}) fusion(bf16[544,128]{1,0:T(8,128)(2,1)S(1)} %copy-done.16, bf16[1,544,1,1,128]{4,1,3,2,0:T(8,128)(2,1)S(1)} %copy.71, pred[544]{0:T(1024)(128)(4,1)} %copy-done.124, pred[544]{0:T(1024)(128)(4,1)S(1)} %get-tuple-element.80, s32[544]{0:T(1024)S(1)} %iota_select_fusion, ...), kind=kOutput, calls=%fused_computation.417 | convolution fusion | flops 78718432 | bytes 1468256 | tf_op jit(solution)/shard_map/csd,ctd->cst/dot_general | solution.py:17
  34.8 1.4 %fusion.276 = (f32[544]{0:T(1024)S(1)}, f32[544,544]{0,1:T(8,128)S(1)}) fusion(bf16[544,128]{1,0:T(8,128)(2,1)S(1)} %copy-done.16, bf16[1,544,1,1,128]{4,1,3,2,0:T(8,128)(2,1)S(1)} %copy.70, pred[544]{0:T(1024)(128)(4,1)S(1)} %copy-done.125, pred[544]{0:T(1024)(128)(4,1)} %copy-done.122, s32[544]{0:T(1024)S(1)} %iota_select_fusion, ...), kind=kOutput, calls=%fused_computation.415 | convolution fusion | flops 78718432 | bytes 1468256 | tf_op jit(solution)/shard_map/csd,ctd->cst/dot_general | solution.py:17
  36.6 0.6 fusion.274
  37.9 0.6 fusion.272
  39.1 0.6 fusion.270
  40.3 0.6 fusion.268
  41.8 0.6 copy-done.89
  42.4 1.0 fusion.229
  43.9 1.0 fusion.231
  45.4 1.0 fusion.233
  47.0 1.0 fusion.235
  48.5 1.0 fusion.237
  50.0 1.0 fusion.239
  51.5 0.6 copy-done.107
  52.1 1.0 fusion.241
  53.0 3.0 %reshape.1316 = bf16[1,544,1,7,128]{4,3,1,2,0:T(8,128)(2,1)} reshape(bf16[544,896]{1,0:T(8,128)(2,1)} %param.8) | data formatting | bytes 1949696 | tf_op jit(solution)/shard_map/reshape | solution.py:111
  56.1 6.1 %fusion.264 = (bf16[1,544,1,1,128]{4,3,1,2,0:T(2,128)(2,1)S(1)}, bf16[1,544,1,1,128]{4,3,1,2,0:T(2,128)(2,1)S(1)}, bf16[1,544,1,1,128]{4,3,1,2,0:T(2,128)(2,1)S(...) fusion(bf16[1,544,1,7,128]{4,3,1,2,0:T(8,128)(2,1)} %reshape.1316), kind=kLoop, calls=%fused_computation.403 | loop fusion | bytes 1949696 | tf_op jit(solution)/shard_map/slice | solution.py:143
  62.7 0.8 copy-done.11
  64.2 0.5 bitcast_dynamic-update-slice_fusion.4
  64.7 0.7 copy-done.5
  66.2 0.5 bitcast_dynamic-update-slice_fusion.2
  67.0 0.5 bitcast_dynamic-update-slice_fusion.1
  67.7 0.5 bitcast_dynamic-update-slice_fusion
  68.1 0.9 copy-done.61
  69.1 0.9 multiply_reduce_fusion
  78.1 0.8 copy.64
  78.9 1.9 %fusion.109 = f32[544,128]{1,0:T(8,128)S(1)} fusion(f32[544,544]{0,1:T(8,128)} %copy-done.13, f32[544]{0:T(1024)S(1)} %copy-done.109, bf16[1,544,1,1,128]{4,1,3,2,0:T(8,128)(2,1)S(1)} %copy-done.60, bf16[544]{0:T(1024)(128)(2,1)S(1)} %get-tuple-element.76), kind=kOutput, calls=%fused_computation.210 | convolution fusion | flops 76421120 | bytes 1604800 | tf_op jit(solution)/shard_map/cst,csd->ctd/dot_general | solution.py:17
  80.9 0.5 fusion.22
  81.4 0.8 copy-done.12
  82.3 0.5 fusion.21
  82.7 0.8 copy-done.9
  84.1 0.8 copy-done.6
  85.0 0.5 fusion.19
  85.4 0.9 copy-done.3
  86.3 0.5 fusion.18
  87.2 0.7 fusion.17
  99.9 1.1 copy.93
  101.8 1.1 copy.94
  102.9 0.9 copy.65
  104.0 0.7 pad_maximum_fusion.1
  104.6 0.7 pad_maximum_fusion
  (363 shorter events, 30.4 us)
Async XLA Ops:
  7.2 95.8 %reduce-scatter.4.cloned.1.call-start = ((), (), s32[]{:S(2)}) async-start(), calls=%async_computation.1 | async-start | bytes 163840
  10.4 21.5 %copy-start.126 = (pred[544]{0:T(1024)(128)(4,1)}, pred[544]{0:T(1024)(128)(4,1)S(1)}, u32[]{:S(2)}) copy-start(pred[544]{0:T(1024)(128)(4,1)S(1)} %fusion.220) | copy-start | bytes 1636
  11.3 20.7 %copy-start.124 = (pred[544]{0:T(1024)(128)(4,1)}, pred[544]{0:T(1024)(128)(4,1)S(1)}, u32[]{:S(2)}) copy-start(pred[544]{0:T(1024)(128)(4,1)S(1)} %get-tuple-element.81) | copy-start | bytes 1636
  11.3 21.3 %copy-start.122 = (pred[544]{0:T(1024)(128)(4,1)}, pred[544]{0:T(1024)(128)(4,1)S(1)}, u32[]{:S(2)}) copy-start(pred[544]{0:T(1024)(128)(4,1)S(1)} %get-tuple-element.80) | copy-start | bytes 1636
  14.1 2.4 %copy-start = (bf16[544,128]{1,0:T(8,128)(2,1)S(1)}, bf16[544,128]{1,0:T(8,128)(2,1)}, u32[]{:S(2)}) copy-start(bf16[544,128]{1,0:T(8,128)(2,1)} %param.7) | copy-start | bytes 417796
  14.2 2.4 %copy-start.16 = (bf16[544,128]{1,0:T(8,128)(2,1)S(1)}, bf16[544,128]{1,0:T(8,128)(2,1)}, u32[]{:S(2)}) copy-start(bf16[544,128]{1,0:T(8,128)(2,1)} %param.6) | copy-start | bytes 417796
  16.6 17.4 %copy-start.29 = (bf16[1,544,1,1,128]{4,1,3,2,0:T(8,128)(2,1)}, bf16[1,544,1,1,128]{4,1,3,2,0:T(8,128)(2,1)S(1)}, u32[]{:S(2)}) copy-start(bf16[1,544,1,1,128]{4,1,3,2,0:T(8,128)(2,1)S(1)} %copy.72) | copy-start | bytes 417796
  31.9 2.4 %copy-start.32 = (bf16[1,544,1,1,128]{4,1,3,2,0:T(8,128)(2,1)}, bf16[1,544,1,1,128]{4,1,3,2,0:T(8,128)(2,1)S(1)}, u32[]{:S(2)}) copy-start(bf16[1,544,1,1,128]{4,1,3,2,0:T(8,128)(2,1)S(1)} %copy.71) | copy-start | bytes 417796
  32.6 2.1 %copy-start.125 = (pred[544]{0:T(1024)(128)(4,1)S(1)}, pred[544]{0:T(1024)(128)(4,1)}, u32[]{:S(2)}) copy-start(pred[544]{0:T(1024)(128)(4,1)} %copy-done.124) | copy-start | bytes 1636
  34.7 9.2 %copy-start.17 = (f32[128,544]{0,1:T(8,128)}, f32[128,544]{0,1:T(8,128)S(1)}, u32[]{:S(2)}) copy-start(f32[128,544]{0,1:T(8,128)S(1)} %get-tuple-element.65) | copy-start | bytes 835588
  36.2 8.7 %copy-start.1 = (f32[544,544]{0,1:T(8,128)}, f32[544,544]{0,1:T(8,128)S(1)}, u32[]{:S(2)}) copy-start(f32[544,544]{0,1:T(8,128)S(1)} %get-tuple-element.61) | copy-start | bytes 3551236
  36.6 8.9 %copy-start.19 = (f32[128,544]{0,1:T(8,128)}, f32[128,544]{0,1:T(8,128)S(1)}, u32[]{:S(2)}) copy-start(f32[128,544]{0,1:T(8,128)S(1)} %get-tuple-element.59) | copy-start | bytes 835588
  37.5 9.0 %copy-start.4 = (f32[544,544]{0,1:T(8,128)}, f32[544,544]{0,1:T(8,128)S(1)}, u32[]{:S(2)}) copy-start(f32[544,544]{0,1:T(8,128)S(1)} %get-tuple-element.55) | copy-start | bytes 3551236
  37.8 9.1 %copy-start.21 = (f32[128,544]{0,1:T(8,128)}, f32[128,544]{0,1:T(8,128)S(1)}, u32[]{:S(2)}) copy-start(f32[128,544]{0,1:T(8,128)S(1)} %get-tuple-element.53) | copy-start | bytes 835588
  38.7 9.2 %copy-start.7 = (f32[544,544]{0,1:T(8,128)}, f32[544,544]{0,1:T(8,128)S(1)}, u32[]{:S(2)}) copy-start(f32[544,544]{0,1:T(8,128)S(1)} %get-tuple-element.49) | copy-start | bytes 3551236
  39.0 9.4 %copy-start.23 = (f32[128,544]{0,1:T(8,128)}, f32[128,544]{0,1:T(8,128)S(1)}, u32[]{:S(2)}) copy-start(f32[128,544]{0,1:T(8,128)S(1)} %get-tuple-element.47) | copy-start | bytes 835588
  39.9 9.5 %copy-start.10 = (f32[544,544]{0,1:T(8,128)}, f32[544,544]{0,1:T(8,128)S(1)}, u32[]{:S(2)}) copy-start(f32[544,544]{0,1:T(8,128)S(1)} %get-tuple-element.43) | copy-start | bytes 3551236
  40.3 9.7 %copy-start.25 = (f32[128,544]{0,1:T(8,128)}, f32[128,544]{0,1:T(8,128)S(1)}, u32[]{:S(2)}) copy-start(f32[128,544]{0,1:T(8,128)S(1)} %get-tuple-element.41) | copy-start | bytes 835588
  40.9 10.0 %copy-start.13 = (f32[544,544]{0,1:T(8,128)}, f32[544,544]{0,1:T(8,128)S(1)}, u32[]{:S(2)}) copy-start(f32[544,544]{0,1:T(8,128)S(1)} %get-tuple-element.37) | copy-start | bytes 3551236
  41.3 10.2 %copy-start.27 = (f32[128,544]{0,1:T(8,128)}, f32[128,544]{0,1:T(8,128)S(1)}, u32[]{:S(2)}) copy-start(f32[128,544]{0,1:T(8,128)S(1)} %get-tuple-element.35) | copy-start | bytes 835588
  56.1 6.2 %copy-start.14 = (f32[544,544]{0,1:T(8,128)S(1)}, f32[544,544]{0,1:T(8,128)}, u32[]{:S(2)}) copy-start(f32[544,544]{0,1:T(8,128)} %copy-done.13) | copy-start | bytes 3551236
  56.1 6.2 %copy-start.69 = (f32[544,128]{1,0:T(8,128)S(1)}, f32[544,128]{1,0:T(8,128)}, u32[]{:S(2)}) copy-start(f32[544,128]{1,0:T(8,128)} %fusion.241) | copy-start | bytes 835588
  56.1 6.2 %copy-start.108 = (f32[544]{0:T(1024)S(1)}, f32[544]{0:T(1024)}, u32[]{:S(2)}) copy-start(f32[544]{0:T(1024)} %copy-done.107) | copy-start | bytes 6532
  70.0 2.6 %copy-start.55 = (bf16[1,544,1,1,128]{4,1,3,2,0:T(8,128)(2,1)}, bf16[1,544,1,1,128]{4,1,3,2,0:T(8,128)(2,1)S(1)}, u32[]{:S(2)}) copy-start(bf16[1,544,1,1,128]{4,1,3,2,0:T(8,128)(2,1)S(1)} %get-tuple-element.14) | copy-start | bytes 417796
  70.0 2.6 %copy-start.57 = (bf16[1,544,1,1,128]{4,1,3,2,0:T(8,128)(2,1)}, bf16[1,544,1,1,128]{4,1,3,2,0:T(8,128)(2,1)S(1)}, u32[]{:S(2)}) copy-start(bf16[1,544,1,1,128]{4,1,3,2,0:T(8,128)(2,1)S(1)} %get-tuple-element.15) | copy-start | bytes 417796
  70.0 2.6 %copy-start.59 = (bf16[1,544,1,1,128]{4,1,3,2,0:T(8,128)(2,1)}, bf16[1,544,1,1,128]{4,1,3,2,0:T(8,128)(2,1)S(1)}, u32[]{:S(2)}) copy-start(bf16[1,544,1,1,128]{4,1,3,2,0:T(8,128)(2,1)S(1)} %get-tuple-element.16) | copy-start | bytes 417796
  70.0 2.6 %copy-start.116 = (f32[544]{0:T(1024)}, f32[544]{0:T(1024)S(1)}, u32[]{:S(2)}) copy-start(f32[544]{0:T(1024)S(1)} %get-tuple-element.7) | copy-start | bytes 6532
  70.0 2.6 %copy-start.118 = (f32[544]{0:T(1024)}, f32[544]{0:T(1024)S(1)}, u32[]{:S(2)}) copy-start(f32[544]{0:T(1024)S(1)} %get-tuple-element.6) | copy-start | bytes 6532
  70.1 2.6 %copy-start.120 = (f32[544]{0:T(1024)}, f32[544]{0:T(1024)S(1)}, u32[]{:S(2)}) copy-start(f32[544]{0:T(1024)S(1)} %get-tuple-element.5) | copy-start | bytes 6532
  70.1 3.1 %copy-start.114 = (f32[544]{0:T(1024)}, f32[544]{0:T(1024)S(1)}, u32[]{:S(2)}) copy-start(f32[544]{0:T(1024)S(1)} %get-tuple-element.8) | copy-start | bytes 6532
  70.1 3.4 %copy-start.53 = (bf16[1,544,1,1,128]{4,1,3,2,0:T(8,128)(2,1)}, bf16[1,544,1,1,128]{4,1,3,2,0:T(8,128)(2,1)S(1)}, u32[]{:S(2)}) copy-start(bf16[1,544,1,1,128]{4,1,3,2,0:T(8,128)(2,1)S(1)} %get-tuple-element.13) | copy-start | bytes 417796
  70.1 3.8 %copy-start.112 = (f32[544]{0:T(1024)}, f32[544]{0:T(1024)S(1)}, u32[]{:S(2)}) copy-start(f32[544]{0:T(1024)S(1)} %get-tuple-element.9) | copy-start | bytes 6532
  70.1 4.2 %copy-start.51 = (bf16[1,544,1,1,128]{4,1,3,2,0:T(8,128)(2,1)}, bf16[1,544,1,1,128]{4,1,3,2,0:T(8,128)(2,1)S(1)}, u32[]{:S(2)}) copy-start(bf16[1,544,1,1,128]{4,1,3,2,0:T(8,128)(2,1)S(1)} %get-tuple-element.12) | copy-start | bytes 417796
  70.1 4.6 %copy-start.110 = (f32[544]{0:T(1024)}, f32[544]{0:T(1024)S(1)}, u32[]{:S(2)}) copy-start(f32[544]{0:T(1024)S(1)} %get-tuple-element.10) | copy-start | bytes 6532
  70.1 4.9 %copy-start.49 = (bf16[1,544,1,1,128]{4,1,3,2,0:T(8,128)(2,1)}, bf16[1,544,1,1,128]{4,1,3,2,0:T(8,128)(2,1)S(1)}, u32[]{:S(2)}) copy-start(bf16[1,544,1,1,128]{4,1,3,2,0:T(8,128)(2,1)S(1)} %get-tuple-element.11) | copy-start | bytes 417796
  70.1 5.7 %copy-start.47 = (bf16[1,544,1,1,128]{4,1,3,2,0:T(8,128)(2,1)}, bf16[1,544,1,1,128]{4,1,3,2,0:T(8,128)(2,1)S(1)}, u32[]{:S(2)}) copy-start(bf16[1,544,1,1,128]{4,1,3,2,0:T(8,128)(2,1)S(1)} %get-tuple-element.17) | copy-start | bytes 417796
  70.1 2.2 %copy-start.24 = (f32[128,544]{0,1:T(8,128)S(1)}, f32[128,544]{0,1:T(8,128)}, u32[]{:S(2)}) copy-start(f32[128,544]{0,1:T(8,128)} %copy-done.23) | copy-start | bytes 835588
  70.9 2.2 %copy-start.22 = (f32[128,544]{0,1:T(8,128)S(1)}, f32[128,544]{0,1:T(8,128)}, u32[]{:S(2)}) copy-start(f32[128,544]{0,1:T(8,128)} %copy-done.21) | copy-start | bytes 835588
  71.9 4.4 %copy-start.77 = (bf16[544,128]{1,0:T(8,128)(2,1)}, bf16[544,128]{1,0:T(8,128)(2,1)S(1)}, u32[]{:S(2)}) copy-start(bf16[544,128]{1,0:T(8,128)(2,1)S(1)} %fusion.62) | copy-start | bytes 417796
  72.7 3.9 %copy-start.79 = (bf16[544,128]{1,0:T(8,128)(2,1)}, bf16[544,128]{1,0:T(8,128)(2,1)S(1)}, u32[]{:S(2)}) copy-start(bf16[544,128]{1,0:T(8,128)(2,1)S(1)} %fusion.63) | copy-start | bytes 417796
  73.5 3.4 %copy-start.81 = (bf16[544,128]{1,0:T(8,128)(2,1)}, bf16[544,128]{1,0:T(8,128)(2,1)S(1)}, u32[]{:S(2)}) copy-start(bf16[544,128]{1,0:T(8,128)(2,1)S(1)} %fusion.64) | copy-start | bytes 417796
  74.3 3.0 %copy-start.83 = (bf16[544,128]{1,0:T(8,128)(2,1)}, bf16[544,128]{1,0:T(8,128)(2,1)S(1)}, u32[]{:S(2)}) copy-start(bf16[544,128]{1,0:T(8,128)(2,1)S(1)} %fusion.65) | copy-start | bytes 417796
  75.1 2.5 %copy-start.85 = (bf16[544,128]{1,0:T(8,128)(2,1)}, bf16[544,128]{1,0:T(8,128)(2,1)S(1)}, u32[]{:S(2)}) copy-start(bf16[544,128]{1,0:T(8,128)(2,1)S(1)} %fusion.66) | copy-start | bytes 417796
  75.1 2.1 %copy-start.36 = (bf16[1,544,1,1,128]{4,1,3,2,0:T(8,128)(2,1)S(1)}, bf16[1,544,1,1,128]{4,1,3,2,0:T(8,128)(2,1)}, u32[]{:S(2)}) copy-start(bf16[1,544,1,1,128]{4,1,3,2,0:T(8,128)(2,1)} %copy-done.35) | copy-start | bytes 417796
  75.8 2.3 %copy-start.87 = (bf16[544,128]{1,0:T(8,128)(2,1)}, bf16[544,128]{1,0:T(8,128)(2,1)S(1)}, u32[]{:S(2)}) copy-start(bf16[544,128]{1,0:T(8,128)(2,1)S(1)} %fusion.67) | copy-start | bytes 417796
  76.6 2.3 %copy-start.60 = (bf16[1,544,1,1,128]{4,1,3,2,0:T(8,128)(2,1)S(1)}, bf16[1,544,1,1,128]{4,1,3,2,0:T(8,128)(2,1)}, u32[]{:S(2)}) copy-start(bf16[1,544,1,1,128]{4,1,3,2,0:T(8,128)(2,1)} %copy-done.59) | copy-start | bytes 417796
  76.6 2.3 %copy-start.109 = (f32[544]{0:T(1024)S(1)}, f32[544]{0:T(1024)}, u32[]{:S(2)}) copy-start(f32[544]{0:T(1024)} %copy-done.107) | copy-start | bytes 6532
  77.8 3.0 %copy-start.121 = (f32[544]{0:T(1024)S(1)}, f32[544]{0:T(1024)}, u32[]{:S(2)}) copy-start(f32[544]{0:T(1024)} %copy-done.120) | copy-start | bytes 6532
  (81 other events, 103.8 us)
Sparse Core Ops, SparseCore 0:
  79.0 20.4 reduce-scatter.3
where the time goes:
time: 113 us; the launch traced here: 112 us
  matrix products  40 us (35%)
  local copies, waits for them, and re-layouts  31.5 us (28%)
  between operations  18.1 us (16%)
  blocking collectives  15.1 us (13%)
  other arithmetic  7.4 us (7%)
    dot_general x84, matrix products, product(): jnp.einsum(pattern, first_arg, second_arg, preferred_element_type=jnp.flo...  40 us
    unnamed x269, local copies, waits for them, and re-layouts  15.5 us
    all_gather x1, blocking collectives, local(): beacon_pairs = lax.all_gather(own_pair, 'span', axis=0, tiled=True)  15.1 us
    slice x1, local copies, waits for them, and re-layouts, local(): grad_blocks[:, :, 0, head_index]  6.13 us
    reshape x1, local copies, waits for them, and re-layouts, local(): grad_blocks = out_grad.reshape(local_spans, SEG, groups, QPG, HD)  3.03 us
    slice x1, local copies, waits for them, and re-layouts, local(): query_blocks[:, :, 0, head_index]  2.37 us
  transfers between devices with their start and end apart: 1, of which 0 were waited for; matrix products, arithmetic and copies ran while one was open for 16% of the time, Pallas kernels for 0%

commit v1 on v0

v1 whole, which is shorter than its diff:
```python
import functools
import math

import jax
import jax.numpy as jnp
from jax import lax
from jax.experimental import pallas as pl
from jax.experimental.pallas import tpu as pltpu
from jax.sharding import PartitionSpec as P

SPAN = 512
HD = 128
BMAX = 32
BLK = 256

SCALE = HD ** (-0.5)
SCALE_LOG2E = SCALE * math.log2(math.e)
FLOOR = -1e30

f32 = jnp.float32
bf16 = jnp.bfloat16


def nt(a, b):
    return lax.dot_general(a, b, (((1,), (1,)), ((), ())), preferred_element_type=f32)


def nn(a, b):
    return lax.dot_general(a, b, (((1,), (0,)), ((), ())), preferred_element_type=f32)


def interleave(blocks):
    waiting, active = list(blocks), []
    while waiting or active:
        if waiting:
            active.append(waiting.pop(0))
        active = [block for block in active if next(block, "end") != "end"]


def kernel(
    n, heads,
    ratios_ref, q_hbm, k_hbm, v_hbm, g_hbm,
    o_hbm, dq_hbm, dk_out, dv_out,
    q_s, g_s, k_s, v_s, kt_s, vt_s, kb_s, vb_s, kbt_s, vbt_s,
    e_s, ot_s, stat_s, bias_s, bbias_s, term_s, recv_s, dk_s, dv_s, o_s, dq_s,
    in_sem, q_sem, g_sem, qb_sem, gb_sem, o_sem, dq_sem, ob_sem, dqb_sem,
    kv_send, kv_recv, term_send, term_recv,
):
    me = lax.axis_index("span")
    chunks = SPAN // BLK
    last = heads * chunks
    nb = n * BMAX

    barrier = pltpu.get_barrier_semaphore()
    for step in range(1, n):
        pl.semaphore_signal(
            barrier, inc=1, device_id={"span": lax.rem(me + step, n)},
            device_id_type=pl.DeviceIdType.MESH,
        )

    def head_cols(h):
        return pl.ds(h * HD, HD)

    def head_rows(h):
        return pl.ds(h * SPAN, SPAN)

    def block_rows(b):
        return pl.ds(b * BLK, BLK)

    def q_copy(h):
        return pltpu.make_async_copy(
            q_hbm.at[pl.ds(0, SPAN), head_cols(h)], q_s.at[head_rows(h)], q_sem.at[h]
        )

    def g_copy(h):
        return pltpu.make_async_copy(
            g_hbm.at[pl.ds(0, SPAN), head_cols(h)], g_s.at[head_rows(h)], g_sem.at[h]
        )

    def tail_copy(src, dst, sem, h):
        return pltpu.make_async_copy(
            src.at[pl.ds(SPAN, BMAX), pl.ds(h * HD, HD)],
            dst.at[pl.ds(last * BLK + h * BMAX, BMAX)],
            sem.at[h],
        )

    k_copy = pltpu.make_async_copy(k_hbm.at[pl.ds(0, SPAN)], k_s, in_sem.at[0])
    v_copy = pltpu.make_async_copy(v_hbm.at[pl.ds(0, SPAN)], v_s, in_sem.at[1])
    mine = pl.ds(pl.multiple_of(me * BMAX, BMAX), BMAX)
    kb_copy = pltpu.make_async_copy(
        k_hbm.at[pl.ds(SPAN, BMAX)], kb_s.at[mine], in_sem.at[2]
    )
    vb_copy = pltpu.make_async_copy(
        v_hbm.at[pl.ds(SPAN, BMAX)], vb_s.at[mine], in_sem.at[3]
    )
    k_copy.start()
    v_copy.start()
    q_copy(0).start()
    kb_copy.start()
    vb_copy.start()
    for h in range(1, heads):
        q_copy(h).start()
    for h in range(heads):
        tail_copy(q_hbm, q_s, qb_sem, h).start()
    for h in range(heads):
        g_copy(h).start()
    for h in range(heads):
        tail_copy(g_hbm, g_s, gb_sem, h).start()

    own_ratio = ratios_ref[me]
    key_id = lax.broadcasted_iota(jnp.int32, (nb, BLK), 0)
    lane_slot = lax.rem(lax.broadcasted_iota(jnp.int32, (nb, BLK), 1), BMAX)
    key_slot = lax.rem(key_id, BMAX)
    key_span = key_id // BMAX
    key_ratio = jnp.zeros((nb, BLK), jnp.int32)
    for s in range(n):
        key_ratio = jnp.where(key_span == s, ratios_ref[s], key_ratio)
    live = (key_slot + 1) * key_ratio <= SPAN
    before = live & (key_span < me)
    bias_s[...] = jnp.where(before, 0.0, FLOOR)
    bbias_s[...] = jnp.where(
        before | (live & (key_span == me) & (key_slot <= lane_slot)), 0.0, FLOOR
    )
    term_s[...] = jnp.zeros_like(term_s)
    dk_s[...] = jnp.zeros_like(dk_s)
    dv_s[...] = jnp.zeros_like(dv_s)
    pad = BLK - heads * BMAX
    q_s[pl.ds(last * BLK + heads * BMAX, pad), :] = jnp.zeros((pad, HD), bf16)
    g_s[pl.ds(last * BLK + heads * BMAX, pad), :] = jnp.zeros((pad, HD), bf16)

    pl.semaphore_wait(barrier, n - 1)

    def kv_copies(step):
        peer = lax.rem(me + step, n)
        return [
            pltpu.make_async_remote_copy(
                src_ref=src.at[pl.ds(SPAN, BMAX)], dst_ref=dst.at[mine],
                send_sem=kv_send.at[i, step - 1], recv_sem=kv_recv.at[i, step - 1],
                device_id={"span": peer}, device_id_type=pl.DeviceIdType.MESH,
            )
            for i, (src, dst) in enumerate(((k_hbm, kb_s), (v_hbm, vb_s)))
        ]

    for step in range(1, n):
        for copy in kv_copies(step):
            copy.start()

    k_copy.wait()
    v_copy.wait()
    kt_s[...] = k_s[...].T
    vt_s[...] = v_s[...].T

    row = lax.broadcasted_iota(jnp.int32, (BLK, BLK), 0)
    col = lax.broadcasted_iota(jnp.int32, (BLK, BLK), 1)

    def own_scores(b, masks, wait=None):
        if wait is not None:
            wait()
        query = q_s[block_rows(b), :]
        scores = nt(k_s[pl.ds(0, len(masks) * BLK), :], query)
        scores = [scores[c * BLK : (c + 1) * BLK] for c in range(len(masks))]
        scores = [
            s if mask is None else jnp.where(mask, s, FLOOR)
            for s, mask in zip(scores, masks)
        ]
        yield
        top = functools.reduce(
            jnp.maximum, [jnp.max(s, axis=0, keepdims=True) for s in scores]
        )
        yield
        total = jnp.zeros((1, BLK), f32)
        parts = []
        for c, s in enumerate(scores):
            e = jnp.exp2((s - top) * SCALE_LOG2E)
            total = total + jnp.sum(e, axis=0, keepdims=True)
            parts.append(e.astype(bf16))
            e_s[b, pl.ds(c * BLK, BLK), :] = parts[-1]
        yield
        mixed = nn(vt_s[:, pl.ds(0, len(masks) * BLK)], jnp.concatenate(parts, 0))
        ot_s[b] = mixed
        stat_s[b, 0:1, :] = top
        stat_s[b, 1:2, :] = total

    reach = (lax.rem(col, BMAX) + 1) * own_ratio

    def tails_in(src, dst, sem):
        for h in range(heads):
            tail_copy(src, dst, sem, h).wait()

    interleave(
        [
            own_scores(
                h * chunks + t, [None] * t + [row <= col],
                q_copy(h).wait if t == 0 else None,
            )
            for h in range(heads)
            for t in range(chunks)
        ]
        + [
            own_scores(
                last, [row + c * BLK < reach for c in range(chunks)],
                functools.partial(tails_in, q_hbm, q_s, qb_sem),
            )
        ]
    )

    kb_copy.wait()
    vb_copy.wait()
    for step in range(1, n):
        for copy in kv_copies(step):
            copy.wait()
    kbt_s[...] = kb_s[...].T
    vbt_s[...] = vb_s[...].T
    ones = jnp.ones((8, HD), bf16)

    def beacon_part(b, bias, live_rows, wait=None, done=None):
        if wait is not None:
            wait()
        query = q_s[block_rows(b), :]
        grad = g_s[block_rows(b), :]
        if live_rows is not None:
            grad = jnp.where(live_rows, grad.astype(f32), 0.0).astype(bf16)
            g_s[block_rows(b), :] = grad
        scores = nt(kb_s[...], query) + bias[...]
        yield
        own_top = stat_s[b, 0:1, :]
        top = jnp.maximum(own_top, jnp.max(scores, axis=0, keepdims=True))
        e = jnp.exp2((scores - top) * SCALE_LOG2E)
        shrink = jnp.exp2((own_top - top) * SCALE_LOG2E)
        total = shrink * stat_s[b, 1:2, :] + jnp.sum(e, axis=0, keepdims=True)
        inverse = 1.0 / total
        factor = shrink * inverse
        probs = e * inverse
        weights = probs.astype(bf16)
        yield
        out = (ot_s[b] * factor + nn(vbt_s[...], weights)).T
        if live_rows is not None:
            out = jnp.where(live_rows, out, 0.0)
        out = out.astype(bf16)
        o_s[block_rows(b), :] = out
        if done is not None:
            done()
        yield
        terms = grad.astype(f32) * out.astype(f32)
        high = terms.astype(bf16)
        low = (terms - high.astype(f32)).astype(bf16)
        delta = (nt(ones, high) + nt(ones, low))[0:1, :]
        slope = nt(vb_s[...], grad)
        yield
        sgrad = (probs * (slope - delta)).astype(bf16)
        yield
        term_s[:, 0:HD] += nn(sgrad, query)
        term_s[:, HD : 2 * HD] += nn(weights, grad)
        ot_s[b] = nn(kbt_s[...], sgrad)
        stat_s[b, 0:1, :] = factor
        stat_s[b, 1:2, :] = delta

    def o_copy(h):
        return pltpu.make_async_copy(
            o_s.at[head_rows(h)], o_hbm.at[pl.ds(0, SPAN), head_cols(h)], o_sem.at[h]
        )

    def dq_copy(h):
        return pltpu.make_async_copy(
            dq_s.at[head_rows(h)], dq_hbm.at[pl.ds(0, SPAN), head_cols(h)], dq_sem.at[h]
        )

    def tail_out(src, dst, sem, h):
        return pltpu.make_async_copy(
            src.at[pl.ds(last * BLK + h * BMAX, BMAX)],
            dst.at[pl.ds(SPAN, BMAX), pl.ds(h * HD, HD)],
            sem.at[h],
        )

    def tails_out(src, dst, sem):
        for h in range(heads):
            tail_out(src, dst, sem, h).start()

    row_slot = lax.rem(lax.broadcasted_iota(jnp.int32, (BLK, HD), 0), BMAX)
    interleave(
        [
            beacon_part(
                h * chunks + t, bias_s, None,
                g_copy(h).wait if t == 0 else None,
                o_copy(h).start if t == chunks - 1 else None,
            )
            for h in range(heads)
            for t in range(chunks)
        ]
        + [
            beacon_part(
                last, bbias_s, (row_slot + 1) * own_ratio <= SPAN,
                functools.partial(tails_in, g_hbm, g_s, gb_sem),
                functools.partial(tails_out, o_s, o_hbm, ob_sem),
            )
        ]
    )

    def own_part(b, count, done=None):
        query = q_s[block_rows(b), :]
        grad = g_s[block_rows(b), :]
        factor = stat_s[b, 0:1, :]
        delta = stat_s[b, 1:2, :]
        keys = pl.ds(0, count * BLK)
        slope = nt(v_s[keys, :], grad)
        yield
        probs = e_s[b, keys, :].astype(f32) * factor
        sgrad = (probs * (slope - delta)).astype(bf16)
        yield
        dk_s[keys, :] += nn(sgrad, query)
        dv_s[keys, :] += nn(probs.astype(bf16), grad)
        dqt = ot_s[b] + nn(kt_s[:, keys], sgrad)
        yield
        dq_s[block_rows(b), :] = (dqt * SCALE).T.astype(bf16)
        if done is not None:
            done()

    def term_copy(step):
        peer = lax.rem(me + step, n)
        return pltpu.make_async_remote_copy(
            src_ref=term_s.at[pl.ds(pl.multiple_of(peer * BMAX, BMAX), BMAX)],
            dst_ref=recv_s.at[step - 1],
            send_sem=term_send.at[step - 1], recv_sem=term_recv.at[step - 1],
            device_id={"span": peer}, device_id_type=pl.DeviceIdType.MESH,
        )

    interleave(
        [own_part(last, chunks, functools.partial(tails_out, dq_s, dq_hbm, dqb_sem))]
    )
    for step in range(1, n):
        term_copy(step).start()

    interleave(
        [
            own_part(
                h * chunks + t, t + 1, dq_copy(h).start if t == chunks - 1 else None
            )
            for h in range(heads)
            for t in range(chunks)
        ]
    )

    dk_out[0:SPAN, :] = (dk_s[...] * SCALE).astype(bf16)
    dv_out[0:SPAN, :] = dv_s[...].astype(bf16)
    total = term_s[mine, :]
    for step in range(1, n):
        term_copy(step).wait()
        total = total + recv_s[step - 1]
    dk_out[SPAN : SPAN + BMAX, :] = (total[:, 0:HD] * SCALE).astype(bf16)
    dv_out[SPAN : SPAN + BMAX, :] = total[:, HD : 2 * HD].astype(bf16)

    for h in range(heads):
        o_copy(h).wait()
        dq_copy(h).wait()
        tail_out(o_s, o_hbm, ob_sem, h).wait()
        tail_out(dq_s, dq_hbm, dqb_sem, h).wait()


def local(n, query_rows, key_rows, value_rows, out_grad, ratios):
    heads = query_rows.shape[1] // HD
    chunks = SPAN // BLK
    blocks = heads * chunks + 1
    nb = n * BMAX
    any_spec = pl.BlockSpec(memory_space=pltpu.HBM)
    vmem_spec = pl.BlockSpec(memory_space=pltpu.VMEM)
    dma = pltpu.SemaphoreType.DMA
    return pl.pallas_call(
        functools.partial(kernel, n, heads),
        out_shape=(
            jax.ShapeDtypeStruct(query_rows.shape, bf16),
            jax.ShapeDtypeStruct(query_rows.shape, bf16),
            jax.ShapeDtypeStruct(key_rows.shape, bf16),
            jax.ShapeDtypeStruct(value_rows.shape, bf16),
        ),
        in_specs=[pl.BlockSpec(memory_space=pltpu.SMEM)] + [any_spec] * 4,
        out_specs=(pl.BlockSpec(memory_space=pl.ANY), pl.BlockSpec(memory_space=pl.ANY), vmem_spec, vmem_spec),
        scratch_shapes=[
            pltpu.VMEM((blocks * BLK, HD), bf16),
            pltpu.VMEM((blocks * BLK, HD), bf16),
            pltpu.VMEM((SPAN, HD), bf16),
            pltpu.VMEM((SPAN, HD), bf16),
            pltpu.VMEM((HD, SPAN), bf16),
            pltpu.VMEM((HD, SPAN), bf16),
            pltpu.VMEM((nb, HD), bf16),
            pltpu.VMEM((nb, HD), bf16),
            pltpu.VMEM((HD, nb), bf16),
            pltpu.VMEM((HD, nb), bf16),
            pltpu.VMEM((blocks, SPAN, BLK), bf16),
            pltpu.VMEM((blocks, HD, BLK), f32),
            pltpu.VMEM((blocks, 8, BLK), f32),
            pltpu.VMEM((nb, BLK), f32),
            pltpu.VMEM((nb, BLK), f32),
            pltpu.VMEM((nb, 2 * HD), f32),
            pltpu.VMEM((n - 1, BMAX, 2 * HD), f32),
            pltpu.VMEM((SPAN, HD), f32),
            pltpu.VMEM((SPAN, HD), f32),
            pltpu.VMEM((blocks * BLK, HD), bf16),
            pltpu.VMEM((blocks * BLK, HD), bf16),
            dma((4,)), dma((heads,)), dma((heads,)), dma((heads,)), dma((heads,)),
            dma((heads,)), dma((heads,)), dma((heads,)), dma((heads,)),
            dma((2, n - 1)), dma((2, n - 1)), dma((n - 1,)), dma((n - 1,)),
        ],
        compiler_params=pltpu.CompilerParams(
            collective_id=0, has_side_effects=True, vmem_limit_bytes=67043328
        ),
        name="beacon_attention",
    )(ratios, query_rows, key_rows, value_rows, out_grad)


def solution(mesh):
    rows = P(("seq", "span"), "kvg")
    return jax.shard_map(
        functools.partial(local, mesh.shape["span"]),
        mesh=mesh,
        in_specs=(rows, rows, rows, rows, P("seq")),
        out_specs=(rows, rows, rows, rows),
        check_vma=False,
    )
```

time: 113 us -> 26.1 us (0.23)
  matrix products: 40 us -> 0 us
  local copies, waits for them, and re-layouts: 31.5 us -> 4.95 us
  Pallas kernels: 0 us -> 20.3 us
  between operations: 18.1 us -> 0.65 us
  blocking collectives: 15.1 us -> 0 us
  other arithmetic: 7.4 us -> 0 us
    dot_general x84 -> x0, matrix products: 40 us -> none  [product(): jnp.einsum(pattern, first_arg, second_arg, preferred_element_type=jnp.flo...]
    pallas_call x0 -> x1, Pallas kernels: none -> 20.3 us  [local(): pl.pallas_call(functools.partial(kernel, n, heads), out_shape=(jax.ShapeD...]
    all_gather x1 -> x0, blocking collectives: 15.1 us -> none  [local(): beacon_pairs = lax.all_gather(own_pair, 'span', axis=0, tiled=True)]
    unnamed x269 -> x10, local copies, waits for them, and re-layouts: 15.5 us -> 4.95 us
    slice x3 -> x0, local copies, waits for them, and re-layouts: 8.51 us -> none  [the longest x1 6.13 us: local(): grad_blocks[:, :, 0, head_index]]
    reshape x3 -> x0, local copies, waits for them, and re-layouts: 5.23 us -> none  [the longest x1 3.03 us: local(): grad_blocks = out_grad.reshape(local_spans, SEG, groups, QPG, HD)]
    reduce_sum x15 -> x0, other arithmetic: 4.37 us -> none  [the longest x7 1.79 us: attend_head(): jnp.sum(jnp.exp(beacon_scores - row_top[..., None]), -1)]
    select_n x2 -> x0, other arithmetic: 1.43 us -> none  [the longest x1 0.78 us: build_masks(): counts = SPAN // ratios]
  transfers between devices with their start and end apart: 1 -> 0, of which waited for: 0 -> 0; matrix products, arithmetic and copies ran while one was open for 16% -> 0% of each run, Pallas kernels for 0% -> 0%
where the time goes in v1:
time: 26.1 us; the launch traced here: 25.9 us
  Pallas kernels  20.3 us (78%)
  local copies, waits for them, and re-layouts  4.95 us (19%)
  between operations  0.65 us (2%)
    pallas_call x1, Pallas kernels, local(): pl.pallas_call(functools.partial(kernel, n, heads), out_shape=(jax.ShapeD...  20.3 us
    unnamed x10, local copies, waits for them, and re-layouts  4.95 us

profile of v1, /device:TPU:0, one launch (start us, length us, event | category | flops | bytes accessed | tf_op | source)
XLA Modules:
  0.0 25.9 jit_solution(14202522102109519323)
XLA Ops:
  0.6 20.3 %beacon_attention.1 = (bf16[544,896]{1,0:T(8,128)(2,1)}, bf16[544,896]{1,0:T(8,128)(2,1)}, bf16[544,128]{1,0:T(8,128)(2,1)}, bf16[544,128]{1,0:T(8,128)(2,1)}) custom-call(s32[4]{0:T(128)} %ratios_ref.1, bf16[544,896]{1,0:T(8,128)(2,1)} %q_hbm.1, bf16[544,128]{1,0:T(8,128)(2,1)} %k_hbm.1, bf16[544,128]{1,0:T(8,128)(2,1)} %v_hbm.1, bf16[544,896]{1,0:T(8,128)(2,1)} %g_hbm.1), custom_call_target="tpu_custom_call" | custom-call | tf_op jit(solution)/shard_map/beacon_attention/pallas_call | solution.py:367
  20.9 0.0 copy-start
  20.9 2.3 %copy.13 = bf16[544,896]{1,0:T(8,128)(2,1)} copy(bf16[544,896]{1,0:T(8,128)(2,1)} %get-tuple-element.8) | data formatting | bytes 1949696
  23.2 0.0 copy-done
  23.2 0.0 copy-start.2
  23.2 0.9 %copy.14 = bf16[544,896]{1,0:T(8,128)(2,1)} copy(bf16[544,896]{1,0:T(8,128)(2,1)S(1)} %copy-done) | data formatting | bytes 1949696
  24.2 0.1 copy-done.2
  24.3 0.0 copy-start.1
  24.3 0.7 %copy.15 = bf16[544,128]{1,0:T(8,128)(2,1)} copy(bf16[544,128]{1,0:T(8,128)(2,1)S(1)} %copy-done.2) | data formatting | bytes 278528
  24.9 0.3 %copy-done.1 = bf16[544,128]{1,0:T(8,128)(2,1)S(1)} copy-done((bf16[544,128]{1,0:T(8,128)(2,1)S(1)}, bf16[544,128]{1,0:T(8,128)(2,1)}, u32[]{:S(2)}) %copy-start.1) | copy-done | bytes 139288
  25.2 0.7 %copy.16 = bf16[544,128]{1,0:T(8,128)(2,1)} copy(bf16[544,128]{1,0:T(8,128)(2,1)S(1)} %copy-done.1) | data formatting | bytes 278528
Async XLA Ops:
  20.9 2.3 %copy-start = (bf16[544,896]{1,0:T(8,128)(2,1)S(1)}, bf16[544,896]{1,0:T(8,128)(2,1)}, u32[]{:S(2)}) copy-start(bf16[544,896]{1,0:T(8,128)(2,1)} %get-tuple-element.9) | copy-start | bytes 2924548
  23.2 1.0 %copy-start.2 = (bf16[544,128]{1,0:T(8,128)(2,1)S(1)}, bf16[544,128]{1,0:T(8,128)(2,1)}, u32[]{:S(2)}) copy-start(bf16[544,128]{1,0:T(8,128)(2,1)} %get-tuple-element.10) | copy-start | bytes 417796
  24.3 1.0 %copy-start.1 = (bf16[544,128]{1,0:T(8,128)(2,1)S(1)}, bf16[544,128]{1,0:T(8,128)(2,1)}, u32[]{:S(2)}) copy-start(bf16[544,128]{1,0:T(8,128)(2,1)} %get-tuple-element.11) | copy-start | bytes 417796
